TPU v7x, 128 devices: a whole 4x4x4 slice. The times are simulated.
128 devices in a mesh: blk: 4 (over x), tok: 32 (over y, z, core).
Axes of the slice: x: 4, y: 4, z: 4, core: 2. Of those that a mesh axis runs over, the one named last changes fastest.
Arguments:
- tokens: bfloat16 [32, 1024, 1664], P('tok', 'blk'), may hold values from -6 to 6
- segment_ids: int32 [32, 1024], P('tok'), may hold values from 0 to 31, as said below
- merge_index: int32 [32, 256, 4], P('tok'), may hold values from 0 to 1023, as said below
- segment_owner: int32 [32, 32], P('tok'), may hold values from 0 to 31, each once within a row
- ln1_gain: float32 [1664], replicated, may hold values from 0.1 to 1.9
- ln1_bias: float32 [1664], replicated, may hold values from -4 to 4
- w_qkv: bfloat16 [3, 1664, 1664], P(None, 'tok', 'blk'), may hold values from -0.15625 to 0.15625
- qkv_bias: float32 [3, 1664], P(None, 'blk'), may hold values from -6 to 6
- w_out: bfloat16 [1664, 1664], P('blk', 'tok'), may hold values from -0.15625 to 0.15625
- out_bias: float32 [1664], replicated, may hold values from -6 to 6
- ln2_gain: float32 [1664], replicated, may hold values from 0.1 to 1.9
- ln2_bias: float32 [1664], replicated, may hold values from -4 to 4
- w_fc1: bfloat16 [1664, 8192], P(None, 'blk'), may hold values from -0.15625 to 0.15625
- fc1_bias: float32 [8192], P('blk'), may hold values from -6 to 6
- w_fc2: bfloat16 [8192, 1664], P('blk'), may hold values from -0.0625 to 0.0625
- fc2_bias: float32 [1664], replicated, may hold values from -6 to 6
- ln3_gain: float32 [1664], replicated, may hold values from 0.1 to 1.9
- ln3_bias: float32 [1664], replicated, may hold values from -4 to 4
- w_proj: bfloat16 [6656, 1664], P('tok', 'blk'), may hold values from -0.078125 to 0.078125
- proj_bias: float32 [1664], P('blk'), may hold values from -6 to 6
Outputs:
- returned: bfloat16 [32, 32, 16, 1664], P('tok', None, None, 'blk')
Inputs may be any that keep to these rules, and one draw needn't show every extreme that they name: `segment_ids`: within a block each segment holds 4 to 64 tokens, one exactly 64; the four tokens of one row of merge_index share a segment. `merge_index`: the rows of one block name each token of the block exactly once. `segment_owner`: each block's row is a permutation of the owners.
All inputs are finite; a program needn't handle non-finite values.
Results may differ from a plain program's by a relative error of at most 0.015.
Values may be sent and summed in bfloat16 or wider, within the bound.
A program may use at most 128 MiB of HBM per device.

v0:
```python
import math
import jax
import jax.numpy as jnp
from jax import lax
from jax.sharding import PartitionSpec as P

HD = 104
EPS = 1e-06


def layer_norm(input_tensors, scales, offset):
    input_tensors = input_tensors.astype(jnp.float32)
    center = input_tensors - jnp.mean(input_tensors, axis=-1, keepdims=True)
    spread = jnp.mean(center * center, axis=-1, keepdims=True)
    return center * lax.rsqrt(spread + EPS) * scales + offset


def body(
    tokens,
    segment_ids,
    merge_index,
    segment_owner,
    ln1_gain,
    ln1_bias,
    w_qkv,
    qkv_bias,
    w_out,
    out_bias,
    ln2_gain,
    ln2_bias,
    w_fc1,
    fc1_bias,
    w_fc2,
    fc2_bias,
    ln3_gain,
    ln3_bias,
    w_proj,
    proj_bias,
):
    tok_block = tokens[0]
    row_count = tok_block.shape[0]
    model_width = tok_block.shape[1]
    head_cols = w_qkv.shape[2]
    heads_here = head_cols // HD
    normed_one = layer_norm(tok_block, ln1_gain, ln1_bias).astype(jnp.bfloat16)
    normed_all = lax.all_gather(normed_one, "blk", axis=0, tiled=True)
    all_rows = normed_all.shape[0]
    columns = normed_all
    projected_qkv = jnp.einsum(
        "td,cde->cte",
        columns,
        lax.all_gather(w_qkv, "tok", axis=1, tiled=True),
        preferred_element_type=jnp.float32,
    )
    projected_qkv = (projected_qkv + qkv_bias[:, None, :]).astype(jnp.bfloat16)
    projected_qkv = projected_qkv.reshape(3, all_rows, heads_here, HD)
    key_rows = projected_qkv[1]
    values = projected_qkv[2]
    segment_row = segment_ids[0]
    q_block = min(512, all_rows)
    block_count = all_rows // q_block
    query_rows = projected_qkv[0].reshape(block_count, q_block, heads_here, HD)
    query_segs = segment_row.reshape(block_count, q_block)
    score_scale = 1.0 / math.sqrt(HD)

    def attend(input_tensors):
        query_part, query_seg = input_tensors
        scores = (
            jnp.einsum("qhe,khe->hqk", query_part, key_rows, preferred_element_type=jnp.float32)
            * score_scale
        )
        allowed = query_seg[:, None] == segment_row[None, :]
        weights = jnp.where(allowed[None], jnp.exp(scores), 0.0)
        attn_probs = (weights / jnp.sum(weights, axis=-1, keepdims=True)).astype(jnp.bfloat16)
        mixed = jnp.einsum("hqk,khe->qhe", attn_probs, values, preferred_element_type=jnp.float32)
        return mixed.astype(jnp.bfloat16)

    attended = lax.map(attend, (query_rows, query_segs)).reshape(all_rows, head_cols)
    out_full = lax.all_gather(w_out, "tok", axis=1, tiled=True)
    attn_rows = lax.psum_scatter(
        jnp.dot(attended, out_full, preferred_element_type=jnp.float32).astype(jnp.bfloat16),
        "blk",
        scatter_dimension=0,
        tiled=True,
    ).astype(jnp.float32)
    after_attn = tok_block.astype(jnp.float32) + attn_rows + out_bias
    normed_two = layer_norm(after_attn, ln2_gain, ln2_bias).astype(jnp.bfloat16)
    pre_act = (
        jnp.dot(
            lax.all_gather(normed_two, "blk", axis=0, tiled=True),
            w_fc1,
            preferred_element_type=jnp.float32,
        )
        + fc1_bias
    )
    hidden_act = jax.nn.gelu(pre_act, approximate=False).astype(jnp.bfloat16)
    partial_sum = jnp.dot(hidden_act, w_fc2, preferred_element_type=jnp.float32)
    own_start = lax.axis_index("blk") * row_count
    own_rows = lax.dynamic_slice_in_dim(partial_sum, own_start, row_count, 0) + after_attn
    partial_sum = lax.dynamic_update_slice_in_dim(partial_sum, own_rows, own_start, 0)
    summed = lax.psum(partial_sum.astype(jnp.bfloat16), "blk").astype(jnp.float32)
    layer_all = (summed + fc2_bias).astype(jnp.bfloat16)
    final_all = layer_norm(layer_all, ln3_gain, ln3_bias).astype(jnp.bfloat16)
    merge_rows = merge_index[0]
    merged_count = merge_rows.shape[0]
    merged = jnp.take(final_all, merge_rows.reshape(-1), axis=0).reshape(
        merged_count, 4 * model_width
    )
    columns = merged
    projected = jnp.dot(
        columns,
        lax.all_gather(w_proj, "tok", axis=0, tiled=True),
        preferred_element_type=jnp.float32,
    )
    projected = (projected + proj_bias).astype(jnp.bfloat16)
    tok_count = lax.axis_size("tok")
    slot_cap = 2 * merged_count // tok_count
    owners_here = segment_owner[0]
    seg_rows = jnp.take(segment_row, merge_rows[:, 0])
    seg_match = (
        seg_rows[:, None] == jnp.arange(owners_here.shape[0], dtype=jnp.int32)[None, :]
    ).astype(jnp.int32)
    owner_rows = jnp.sum(seg_match * owners_here[None, :], axis=1)
    segment_matches = (
        owner_rows[:, None] == jnp.arange(tok_count, dtype=jnp.int32)[None, :]
    ).astype(jnp.int32)
    before = jnp.cumsum(segment_matches, axis=0) - segment_matches
    order_in = jnp.sum(before * segment_matches, axis=1)
    target = owner_rows * slot_cap + order_in
    placed = (jnp.arange(tok_count * slot_cap, dtype=jnp.int32)[:, None] == target[None, :]).astype(
        jnp.bfloat16
    )
    outgoing = jnp.dot(placed, projected, preferred_element_type=jnp.float32).astype(jnp.bfloat16)
    outgoing = outgoing.reshape(tok_count, slot_cap, projected.shape[1])
    arrived = lax.all_to_all(outgoing, "tok", split_axis=0, concat_axis=0, tiled=True)
    return arrived[None]


def solution(mesh):
    placed = (
        P("tok", "blk", None),
        P("tok", None),
        P("tok", None, None),
        P("tok", None),
        P(),
        P(),
        P(None, "tok", "blk"),
        P(None, "blk"),
        P("blk", "tok"),
        P(),
        P(),
        P(),
        P(None, "blk"),
        P("blk"),
        P("blk", None),
        P(),
        P(),
        P(),
        P("tok", "blk"),
        P("blk"),
    )
    return jax.shard_map(
        body, mesh=mesh, in_specs=placed, out_specs=P("tok", None, None, "blk"), check_vma=False
    )
```

profile of v0, /device:TPU:1, one launch (start us, length us, event | category | flops | bytes accessed | tf_op | source)
XLA Modules:
  0.0 480.8 jit_solution(5821261523930769322)
XLA Ops:
  16.4 40.5 %all-gather.15.cloned.1.call-done = bf16[32,52,416]{2,1,0:T(8,128)(2,1)} async-done(((bf16[1,52,416]{2,1,0:T(8,128)(2,1)}), bf16[32,52,416]{2,1,0:T(8,128)(2,1)}) %all-gather.15.cloned.1.call-update) | async-done | bytes 1384464 | tf_op jit(solution)/shard_map/all_gather | solution.py:79
  56.9 2.7 reshape.179
  59.7 39.4 %all-gather.7.cloned.1.call-done = bf16[1024,1664]{1,0:T(8,128)(2,1)} async-done(((bf16[256,1664]{1,0:T(8,128)(2,1)}), bf16[1024,1664]{1,0:T(8,128)(2,1)}) %all-gather.7.cloned.1.call-update) | async-done | bytes 3407888 | tf_op jit(solution)/shard_map/all_gather | solution.py:46
  99.1 53.1 %all-gather.9.cloned.1.call-done = bf16[3,1664,416]{2,0,1:T(4,128)(2,1)} async-done(((bf16[3,52,416]{2,0,1:T(4,128)(2,1)}), bf16[3,1664,416]{2,0,1:T(4,128)(2,1)}) %all-gather.9.cloned.1.call-update) | async-done | bytes 4153360 | tf_op jit(solution)/shard_map/all_gather | solution.py:52
  152.2 9.2 %fusion.34 = bf16[3,1024,416]{1,2,0:T(8,128)(2,1)S(1)} fusion(f32[3,416]{1,0:T(4,128)S(1)} %copy-done.15, bf16[3,1664,416]{2,0,1:T(4,128)(2,1)} %all-gather.9.cloned.1.call-done, bf16[1024,1664]{1,0:T(8,128)(2,1)} %all-gather.7.cloned.1.call-done), kind=kOutput, calls=%fused_computation.53 | convolution fusion | flops 4255580160 | bytes 10122112 | tf_op jit(solution)/shard_map/td,cde->cte/dot_general | solution.py:49
  164.4 15.8 %while.10 = (s32[]{:T(128)}, bf16[2,512,4,104]{1,3,2,0:T(8,128)(2,1)}, s32[2,512]{1,0:T(2,128)S(1)}, s32[1,1024]{1,0:T(1,128)S(1)}, bf16[2,512,4,104]{1,3,2,0:T(...) while((s32[]{:T(128)}, bf16[2,512,4,104]{1,3,2,0:T(8,128)(2,1)}, ...), condition=%wide.region_8.9_spmd, body=%wide.region_6.8_spmd.sunk | while | flops 887830528 | bytes 31156912 | solution.py:78
  164.8 4.0 fusion.112
  168.8 2.5 fusion.113
  172.6 4.0 fusion.112
  176.6 2.5 fusion.113
  182.4 3.9 convolution_convert_fusion
  186.4 38.9 %reduce-scatter.2.cloned.1.call-done = bf16[256,1664]{1,0:T(8,128)(2,1)} async-done(((bf16[1024,1664]{1,0:T(8,128)(2,1)}), bf16[256,1664]{1,0:T(8,128)(2,1)}) %reduce-scatter.2.cloned.1.call-update) | async-done | bytes 851984 | tf_op jit(solution)/shard_map/reduce_scatter | solution.py:80
  228.5 2.6 add_convert_fusion.2
  231.3 41.5 %all-gather.11.cloned.1.call-done = bf16[1024,1664]{1,0:T(8,128)(2,1)} async-done(((bf16[256,1664]{1,0:T(8,128)(2,1)}), bf16[1024,1664]{1,0:T(8,128)(2,1)}) %all-gather.11.cloned.1.call-update) | async-done | bytes 3407888 | tf_op jit(solution)/shard_map/all_gather | solution.py:90
  272.7 11.1 %fusion.97 = f32[1024,2048]{1,0:T(8,128)S(1)} fusion(bf16[1024,1664]{1,0:T(8,128)(2,1)} %all-gather.11.cloned.1.call-done, bf16[1664,2048]{1,0:T(8,128)(2,1)} %param.34), kind=kOutput, calls=%fused_computation.133 | convolution fusion | flops 6979321856 | bytes 18612224 | tf_op jit(solution)/shard_map/dot_general | solution.py:89
  283.9 28.8 %fusion.29 = f32[1024,1664]{1,0:T(8,128)S(1)} fusion(bf16[2048,1664]{1,0:T(8,128)(2,1)} %param.36, f32[1024,2048]{1,0:T(8,128)S(1)} %fusion.97, f32[2048]{0:T(1024)S(1)} %copy-done.16), kind=kOutput, calls=%fused_computation.48 | convolution fusion | flops 7117733888 | bytes 22028288 | tf_op jit(solution)/shard_map/dot_general | solution.py:97
  322.1 73.7 %all-reduce.2.cloned.1.call-done = bf16[1024,1664]{1,0:T(8,128)(2,1)} async-done(((bf16[1024,1664]{1,0:T(8,128)(2,1)}), bf16[1024,1664]{1,0:T(8,128)(2,1)}) %all-reduce.2.cloned.1.call-update) | async-done | bytes 3407888 | tf_op jit(solution)/shard_map/psum | solution.py:101
  395.8 2.8 convert_reduce_fusion
  398.7 3.2 fusion.23
  403.7 5.9 %gather_fusion.1 = bf16[1024,1664]{1,0:T(8,128)(2,1)} fusion(bf16[1024,1664]{1,0:T(8,128)(2,1)S(1)} %fusion.26, s32[1024]{0:T(1024)S(1)} %broadcast_clamp_fusion), kind=kCustom, calls=%fused_computation.1 | custom fusion | bytes 6819840 | tf_op jit(solution)/shard_map/jit(_take)/gather | solution.py:106
  409.6 5.4 %gather.15 = bf16[256,6656]{1,0:T(8,128)(2,1)S(1)} reshape(bf16[1024,1664]{1,0:T(8,128)(2,1)} %gather_fusion.1) | data formatting | bytes 6815744 | tf_op jit(solution)/shard_map/jit(_take)/gather | solution.py:106
  415.0 33.5 %all-gather.13.cloned.1.call-done = bf16[6656,416]{1,0:T(8,128)(2,1)} async-done(((bf16[208,416]{1,0:T(8,128)(2,1)}), bf16[6656,416]{1,0:T(8,128)(2,1)}) %all-gather.13.cloned.1.call-update) | async-done | bytes 5537808 | tf_op jit(solution)/shard_map/all_gather | solution.py:112
  448.5 7.0 %convolution_convert_fusion.1 = bf16[512,416]{0,1:T(8,128)(2,1)} fusion(bf16[6656,416]{1,0:T(8,128)(2,1)} %all-gather.13.cloned.1.call-done, pred[256,6656]{1,0:T(8,128)(4,1)} %bitcast.118, bf16[256,6656]{1,0:T(8,128)(2,1)S(1)} %gather.15, s32[256]{0:T(256)S(1)} %multiply_add_fusion, f32[416]{0:T(512)S(1)} %copy-done.17), kind=kOutput, calls=%fused_computation.69 | convolution fusion | flops 1528987648 | bytes 11078272 | tf_op jit(solution)/shard_map/dot_general | solution.py:133
  456.7 16.2 %all_to_all.5 = bf16[32,16,416]{2,1,0:T(8,128)(2,1)S(1)} all-to-all(bf16[32,16,416]{2,1,0:T(8,128)(2,1)S(1)} %bitcast.116), channel_id=1, replica_groups=mesh['blk'=4,'tok'=32] {'tok'}, dimensions={0} | all-to-all | bytes 851968 | tf_op jit(solution)/shard_map/all_to_all | solution.py:135
  (106 shorter events, 34.0 us)
Async XLA Ops:
  6.5 145.7 %copy-start.15 = (f32[3,416]{1,0:T(4,128)S(1)}, f32[3,416]{1,0:T(4,128)}, u32[]{:S(2)}) copy-start(f32[3,416]{1,0:T(4,128)} %param.29) | copy-start | bytes 14980
  6.5 50.4 %all-gather.15.cloned.1.call-start = ((), (), s32[]{:S(2)}) async-start(), calls=%async_computation.8 | async-start | bytes 1892352 | tf_op jit(solution)/shard_map/all_gather | solution.py:79
  7.3 91.8 %all-gather.7.cloned.1.call-start = ((), (), s32[]{:S(2)}) async-start(), calls=%async_computation.2 | async-start | bytes 4259840 | tf_op jit(solution)/shard_map/all_gather | solution.py:46
  12.8 139.4 %all-gather.9.cloned.1.call-start = ((), (), s32[]{:S(2)}) async-start(), calls=%async_computation.3 | async-start | bytes 7028736 | tf_op jit(solution)/shard_map/all_gather | solution.py:52
  14.5 210.8 %reduce-scatter.2.cloned.1.call-start = ((), (), s32[]{:S(2)}) async-start(), calls=%async_computation.4 | async-start | bytes 4259840 | tf_op jit(solution)/shard_map/reduce_scatter | solution.py:80
  164.4 4.3 copy-start.4
  164.4 4.3 copy-start.5
  172.2 4.3 copy-start.4
  172.2 4.3 copy-start.5
  182.4 42.9 %copy-start.1 = (bf16[1,256,1664]{2,1,0:T(8,128)(2,1)S(1)}, bf16[1,256,1664]{2,1,0:T(8,128)(2,1)}, u32[]{:S(2)}) copy-start(bf16[1,256,1664]{2,1,0:T(8,128)(2,1)} %param.22) | copy-start | bytes 2555908
  182.4 42.9 %copy-start.7 = (f32[1664]{0:T(1024)S(1)}, f32[1664]{0:T(1024)}, u32[]{:S(2)}) copy-start(f32[1664]{0:T(1024)} %param.31) | copy-start | bytes 19972
  186.4 42.2 %copy-start.10 = (f32[1664]{0:T(1024)S(1)}, f32[1664]{0:T(1024)}, u32[]{:S(2)}) copy-start(f32[1664]{0:T(1024)} %param.33) | copy-start | bytes 19972
  186.4 42.2 %copy-start.11 = (f32[1664]{0:T(1024)S(1)}, f32[1664]{0:T(1024)}, u32[]{:S(2)}) copy-start(f32[1664]{0:T(1024)} %param.32) | copy-start | bytes 19972
  186.4 86.3 %all-gather.11.cloned.1.call-start = ((), (), s32[]{:S(2)}) async-start(), calls=%async_computation.5 | async-start | bytes 4259840 | tf_op jit(solution)/shard_map/all_gather | solution.py:90
  231.2 164.6 %all-reduce.2.cloned.1.call-start = ((), (), s32[]{:S(2)}) async-start(), calls=%async_computation.6 | async-start | bytes 6815744 | tf_op jit(solution)/shard_map/psum | solution.py:101
  231.2 52.6 %copy-start.16 = (f32[2048]{0:T(1024)S(1)}, f32[2048]{0:T(1024)}, u32[]{:S(2)}) copy-start(f32[2048]{0:T(1024)} %param.35) | copy-start | bytes 24580
  283.9 28.9 %copy-start.3 = (bf16[256,1664]{1,0:T(8,128)(2,1)S(1)}, bf16[256,1664]{1,0:T(8,128)(2,1)}, u32[]{:S(2)}) copy-start(bf16[256,1664]{1,0:T(8,128)(2,1)} %reduce-scatter.2.cloned.1.call-done) | copy-start | bytes 2555908
  313.2 4.7 copy-start.14
  315.4 80.4 %copy-start.8 = (f32[1664]{0:T(1024)S(1)}, f32[1664]{0:T(1024)}, u32[]{:S(2)}) copy-start(f32[1664]{0:T(1024)} %param.37) | copy-start | bytes 19972
  315.4 133.1 %all-gather.13.cloned.1.call-start = ((), (), s32[]{:S(2)}) async-start(), calls=%async_computation.7 | async-start | bytes 7028736 | tf_op jit(solution)/shard_map/all_gather | solution.py:112
  316.2 85.7 %copy-start.12 = (f32[1664]{0:T(1024)S(1)}, f32[1664]{0:T(1024)}, u32[]{:S(2)}) copy-start(f32[1664]{0:T(1024)} %param.39) | copy-start | bytes 19972
  316.2 85.6 %copy-start.13 = (f32[1664]{0:T(1024)S(1)}, f32[1664]{0:T(1024)}, u32[]{:S(2)}) copy-start(f32[1664]{0:T(1024)} %param.38) | copy-start | bytes 19972
  395.8 6.1 %copy-start.2 = (bf16[1024,1664]{1,0:T(8,128)(2,1)S(1)}, bf16[1024,1664]{1,0:T(8,128)(2,1)}, u32[]{:S(2)}) copy-start(bf16[1024,1664]{1,0:T(8,128)(2,1)} %all-reduce.2.cloned.1.call-done) | copy-start | bytes 10223620
  409.6 39.0 %copy-start.17 = (f32[416]{0:T(512)S(1)}, f32[416]{0:T(512)}, u32[]{:S(2)}) copy-start(f32[416]{0:T(512)} %param.41) | copy-start | bytes 4996
  (4 other events, 7.9 us)
Sparse Core Ops, SparseCore 0:
  9.6 47.2 all-gather.14
  58.6 40.4 all-gather.6
  101.3 50.8 all-gather.8
  186.5 38.7 reduce-scatter.1
  231.3 41.3 all-gather.10
  315.5 80.1 all-reduce.1
  398.0 50.4 all-gather.12
where the time goes:
time: 490 us; the launch traced here: 481 us
  waiting for transfers between devices  322 us (66%)
  matrix products  73 us (15%)
  local copies, waits for them, and re-layouts  30.3 us (6%)
  other arithmetic  24.6 us (5%)
  blocking collectives  16.2 us (3%)
  between operations  14 us (3%)
    psum x1, waiting for transfers between devices, body(): lax.psum(partial_sum.astype(jnp.bfloat16), 'blk').astype(jnp.float32)  73.7 us
    all_gather x1, waiting for transfers between devices, body(): lax.all_gather(w_qkv, 'tok', axis=1, tiled=True)  53.1 us
    all_gather x1, waiting for transfers between devices, body(): lax.all_gather(normed_two, 'blk', axis=0, tiled=True)  41.5 us
    all_gather x1, waiting for transfers between devices, body(): out_full = lax.all_gather(w_out, 'tok', axis=1, tiled=True)  40.5 us
    all_gather x1, waiting for transfers between devices, body(): normed_all = lax.all_gather(normed_one, 'blk', axis=0, tiled=True)  39.4 us
    reduce_scatter x1, waiting for transfers between devices, body(): lax.psum_scatter(jnp.dot(attended, out_full, preferred_element_type=jnp.f...  38.9 us
    all_gather x1, waiting for transfers between devices, body(): lax.all_gather(w_proj, 'tok', axis=0, tiled=True)  33.5 us
    dot_general x1, matrix products, body(): partial_sum = jnp.dot(hidden_act, w_fc2, preferred_element_type=jnp.float32)  28.8 us
  transfers between devices with their start and end apart: 7, of which 7 were waited for; matrix products, arithmetic and copies ran while one was open for 8% of the time, Pallas kernels for 0%

commit v1 on v0

--- a/solution.py
+++ b/solution.py
@@ -6,6 +6,19 @@
 
 HD = 104
 EPS = 1e-06
+
+
+def collect(shard, axis, dim):
+    ways = lax.axis_size(axis)
+    up = [(d, (d + 1) % ways) for d in range(ways)]
+    down = [(d, (d - 1) % ways) for d in range(ways)]
+    earlier, later = ([shard], [shard])
+    for _ in range(ways // 2):
+        earlier.append(lax.ppermute(earlier[-1], axis, up))
+    for _ in range((ways - 1) // 2):
+        later.append(lax.ppermute(later[-1], axis, down))
+    line = jnp.concatenate([*earlier[::-1], *later[1:]], axis=dim)
+    return jnp.roll(line, (lax.axis_index(axis) - ways // 2) * shard.shape[dim], axis=dim)
 
 
 def layer_norm(input_tensors, scales, offset):
@@ -43,7 +56,7 @@
     head_cols = w_qkv.shape[2]
     heads_here = head_cols // HD
     normed_one = layer_norm(tok_block, ln1_gain, ln1_bias).astype(jnp.bfloat16)
-    normed_all = lax.all_gather(normed_one, "blk", axis=0, tiled=True)
+    normed_all = collect(normed_one, "blk", 0)
     all_rows = normed_all.shape[0]
     columns = normed_all
     projected_qkv = jnp.einsum(

time: 490 us -> 439 us (0.90); the launches traced: 481 us -> 436 us
  waiting for transfers between devices: 322 us -> 264 us
  local copies, waits for them, and re-layouts: 30.3 us -> 35.3 us
    all_gather x1, waiting for transfers between devices: 40.5 us -> 0.01 us  [body(): out_full = lax.all_gather(w_out, 'tok', axis=1, tiled=True)]
    all_gather x1 -> x0, waiting for transfers between devices: 39.4 us -> none  [body(): normed_all = lax.all_gather(normed_one, 'blk', axis=0, tiled=True)]
    ppermute x0 -> x3, waiting for transfers between devices: none -> 35 us  [the longest x2 35 us: collect(): earlier.append(lax.ppermute(earlier[-1], axis, up))]
    all_gather x1, waiting for transfers between devices: 53.1 us -> 39.9 us  [body(): lax.all_gather(w_qkv, 'tok', axis=1, tiled=True)]
    unnamed x37 -> x48, local copies, waits for them, and re-layouts: 8.1 us -> 14.2 us
  transfers between devices with their start and end apart: 7 -> 9, of which waited for: 7 -> 7; matrix products, arithmetic and copies ran while one was open for 8% -> 11% of each run, Pallas kernels for 0% -> 0%
where the time goes in v1:
time: 439 us; the launch traced here: 436 us
  waiting for transfers between devices  264 us (60%)
  matrix products  74.3 us (17%)
  local copies, waits for them, and re-layouts  35.3 us (8%)
  other arithmetic  27.2 us (6%)
  blocking collectives  16.2 us (4%)
  between operations  14.1 us (3%)
  starting transfers between devices  5.08 us (1%)
    psum x1, waiting for transfers between devices, body(): lax.psum(partial_sum.astype(jnp.bfloat16), 'blk').astype(jnp.float32)  73.9 us
    all_gather x1, waiting for transfers between devices, body(): lax.all_gather(normed_two, 'blk', axis=0, tiled=True)  41.5 us
    all_gather x1, waiting for transfers between devices, body(): lax.all_gather(w_qkv, 'tok', axis=1, tiled=True)  39.9 us
    reduce_scatter x1, waiting for transfers between devices, body(): lax.psum_scatter(jnp.dot(attended, out_full, preferred_element_type=jnp.f...  38.9 us
    ppermute x2, waiting for transfers between devices, collect(): earlier.append(lax.ppermute(earlier[-1], axis, up))  35 us
    all_gather x1, waiting for transfers between devices, body(): lax.all_gather(w_proj, 'tok', axis=0, tiled=True)  33.4 us
    dot_general x1, matrix products, body(): partial_sum = jnp.dot(hidden_act, w_fc2, preferred_element_type=jnp.float32)  28.6 us
    all_to_all x1, blocking collectives, body(): lax.all_to_all(outgoing, 'tok', split_axis=0, concat_axis=0, tiled=True)  16.2 us
  transfers between devices with their start and end apart: 9, of which 7 were waited for; matrix products, arithmetic and copies ran while one was open for 11% of the time, Pallas kernels for 0%

profile of v1, /device:TPU:1, one launch (start us, length us, event | category | flops | bytes accessed | tf_op | source)
XLA Modules:
  0.0 436.2 jit_solution(10292976960894705226)
XLA Ops:
  16.5 19.7 %collective-permute-done = bf16[256,1664]{1,0:T(8,128)(2,1)S(1)} collective-permute-done((bf16[256,1664]{1,0:T(8,128)(2,1)}, bf16[256,1664]{1,0:T(8,128)(2,1)S(1)}, u32[]{:S(2)}, u32[]{:S(2)}) %collective-permute-start) | collective-permute-done | bytes 852000 | tf_op jit(solution)/shard_map/ppermute | solution.py:17
  40.9 15.3 %collective-permute-done.1 = bf16[256,1664]{1,0:T(8,128)(2,1)S(1)} collective-permute-done((bf16[256,1664]{1,0:T(8,128)(2,1)S(1)}, bf16[256,1664]{1,0:T(8,128)(2,1)S(1)}, u32[]{:S(2)}, u32[]{:S(2)}) %collective-permute-start.1) | collective-permute-done | bytes 852000 | tf_op jit(solution)/shard_map/ppermute | solution.py:17
  64.8 3.9 reshape.179
  68.7 39.9 %all-gather.6.cloned.1.call-done = bf16[3,1664,416]{2,0,1:T(4,128)(2,1)} async-done(((bf16[3,52,416]{2,0,1:T(4,128)(2,1)}), bf16[3,1664,416]{2,0,1:T(4,128)(2,1)}) %all-gather.6.cloned.1.call-update) | async-done | bytes 4153360 | tf_op jit(solution)/shard_map/all_gather | solution.py:65
  108.6 9.2 %fusion.35 = bf16[3,1024,416]{1,2,0:T(8,128)(2,1)S(1)} fusion(f32[3,416]{1,0:T(4,128)S(1)} %copy-done.15, bf16[3,1664,416]{2,0,1:T(4,128)(2,1)} %all-gather.6.cloned.1.call-done, bf16[2048,1664]{1,0:T(8,128)(2,1)} %constant_dynamic-update-slice_fusion, s32[]{:T(128)S(6)} %select_n.59), kind=kOutput, calls=%fused_computation.54 | convolution fusion | flops 4255580160 | bytes 12784516 | tf_op jit(solution)/shard_map/td,cde->cte/dot_general | solution.py:62
  120.5 15.2 %while.10 = (s32[]{:T(128)}, bf16[2,512,4,104]{1,3,2,0:T(8,128)(2,1)}, s32[2,512]{1,0:T(2,128)S(1)}, s32[1,1024]{1,0:T(1,128)S(1)}, bf16[2,512,4,104]{1,3,2,0:T(...) while((s32[]{:T(128)}, bf16[2,512,4,104]{1,3,2,0:T(8,128)(2,1)}, ...), condition=%wide.region_8.9_spmd, body=%wide.region_6.8_spmd.sunk | while | flops 887830528 | bytes 20933720 | solution.py:91
  120.9 4.0 fusion.114
  124.9 3.2 fusion.115
  128.5 3.8 fusion.114
  132.3 3.2 fusion.115
  138.0 3.9 convolution_convert_fusion
  142.0 38.9 %reduce-scatter.2.cloned.1.call-done = bf16[256,1664]{1,0:T(8,128)(2,1)} async-done(((bf16[1024,1664]{1,0:T(8,128)(2,1)}), bf16[256,1664]{1,0:T(8,128)(2,1)}) %reduce-scatter.2.cloned.1.call-update) | async-done | bytes 851984 | tf_op jit(solution)/shard_map/reduce_scatter | solution.py:93
  184.1 2.6 add_convert_fusion.2
  186.8 41.5 %all-gather.8.cloned.1.call-done = bf16[1024,1664]{1,0:T(8,128)(2,1)} async-done(((bf16[256,1664]{1,0:T(8,128)(2,1)}), bf16[1024,1664]{1,0:T(8,128)(2,1)}) %all-gather.8.cloned.1.call-update) | async-done | bytes 3407888 | tf_op jit(solution)/shard_map/all_gather | solution.py:103
  228.3 11.3 %fusion.99 = f32[1024,2048]{1,0:T(8,128)S(1)} fusion(bf16[1024,1664]{1,0:T(8,128)(2,1)} %all-gather.8.cloned.1.call-done, bf16[1664,2048]{1,0:T(8,128)(2,1)} %param.34), kind=kOutput, calls=%fused_computation.143 | convolution fusion | flops 6979321856 | bytes 18612224 | tf_op jit(solution)/shard_map/dot_general | solution.py:102
  239.6 28.6 %fusion.29 = f32[1024,1664]{1,0:T(8,128)S(1)} fusion(bf16[2048,1664]{1,0:T(8,128)(2,1)} %param.36, f32[1024,2048]{1,0:T(8,128)S(1)} %fusion.99, f32[2048]{0:T(1024)S(1)} %copy-done.16), kind=kOutput, calls=%fused_computation.48 | convolution fusion | flops 7117733888 | bytes 22028288 | tf_op jit(solution)/shard_map/dot_general | solution.py:110
  277.5 73.9 %all-reduce.2.cloned.1.call-done = bf16[1024,1664]{1,0:T(8,128)(2,1)} async-done(((bf16[1024,1664]{1,0:T(8,128)(2,1)}), bf16[1024,1664]{1,0:T(8,128)(2,1)}) %all-reduce.2.cloned.1.call-update) | async-done | bytes 3407888 | tf_op jit(solution)/shard_map/psum | solution.py:114
  351.3 2.8 convert_reduce_fusion
  354.2 3.2 fusion.23
  359.3 5.9 %gather_fusion.1 = bf16[1024,1664]{1,0:T(8,128)(2,1)} fusion(bf16[1024,1664]{1,0:T(8,128)(2,1)S(1)} %fusion.26, s32[1024]{0:T(1024)S(1)} %broadcast_clamp_fusion), kind=kCustom, calls=%fused_computation.1 | custom fusion | bytes 6819840 | tf_op jit(solution)/shard_map/jit(_take)/gather | solution.py:119
  365.1 5.4 %gather.15 = bf16[256,6656]{1,0:T(8,128)(2,1)S(1)} reshape(bf16[1024,1664]{1,0:T(8,128)(2,1)} %gather_fusion.1) | data formatting | bytes 6815744 | tf_op jit(solution)/shard_map/jit(_take)/gather | solution.py:119
  370.6 33.4 %all-gather.10.cloned.1.call-done = bf16[6656,416]{1,0:T(8,128)(2,1)} async-done(((bf16[208,416]{1,0:T(8,128)(2,1)}), bf16[6656,416]{1,0:T(8,128)(2,1)}) %all-gather.10.cloned.1.call-update) | async-done | bytes 5537808 | tf_op jit(solution)/shard_map/all_gather | solution.py:125
  403.9 7.0 %convolution_convert_fusion.1 = bf16[512,416]{0,1:T(8,128)(2,1)} fusion(bf16[6656,416]{1,0:T(8,128)(2,1)} %all-gather.10.cloned.1.call-done, pred[256,6656]{1,0:T(8,128)(4,1)} %bitcast.122, bf16[256,6656]{1,0:T(8,128)(2,1)S(1)} %gather.15, s32[256]{0:T(256)S(1)} %multiply_add_fusion, f32[416]{0:T(512)S(1)} %copy-done.17), kind=kOutput, calls=%fused_computation.70 | convolution fusion | flops 1528987648 | bytes 11078272 | tf_op jit(solution)/shard_map/dot_general | solution.py:146
  412.1 16.2 %all_to_all.5 = bf16[32,16,416]{2,1,0:T(8,128)(2,1)S(1)} all-to-all(bf16[32,16,416]{2,1,0:T(8,128)(2,1)S(1)} %bitcast.120), channel_id=1, replica_groups=mesh['blk'=4,'tok'=32] {'tok'}, dimensions={0} | all-to-all | bytes 851968 | tf_op jit(solution)/shard_map/all_to_all | solution.py:148
  (111 shorter events, 45.2 us)
Async XLA Ops:
  6.5 51.6 %copy-start.1 = (bf16[1,256,1664]{2,1,0:T(8,128)(2,1)S(1)}, bf16[1,256,1664]{2,1,0:T(8,128)(2,1)}, u32[]{:S(2)}) copy-start(bf16[1,256,1664]{2,1,0:T(8,128)(2,1)} %param.22) | copy-start | bytes 2555908
  6.5 51.6 %copy-start.7 = (f32[1664]{0:T(1024)S(1)}, f32[1664]{0:T(1024)}, u32[]{:S(2)}) copy-start(f32[1664]{0:T(1024)} %param.26) | copy-start | bytes 19972
  6.5 51.6 %copy-start.6 = (f32[1664]{0:T(1024)S(1)}, f32[1664]{0:T(1024)}, u32[]{:S(2)}) copy-start(f32[1664]{0:T(1024)} %param.27) | copy-start | bytes 19972
  6.5 58.3 %all-gather.12.cloned.1.call-start = ((), (), s32[]{:S(2)}) async-start(), calls=%async_computation.7 | async-start | bytes 1892352 | tf_op jit(solution)/shard_map/all_gather | solution.py:92
  7.3 101.3 %all-gather.6.cloned.1.call-start = ((), (), s32[]{:S(2)}) async-start(), calls=%async_computation.2 | async-start | bytes 7028736 | tf_op jit(solution)/shard_map/all_gather | solution.py:65
  9.0 171.8 %reduce-scatter.2.cloned.1.call-start = ((), (), s32[]{:S(2)}) async-start(), calls=%async_computation.3 | async-start | bytes 4259840 | tf_op jit(solution)/shard_map/reduce_scatter | solution.py:93
  14.5 21.7 %collective-permute-start = (bf16[256,1664]{1,0:T(8,128)(2,1)}, bf16[256,1664]{1,0:T(8,128)(2,1)S(1)}, u32[]{:S(2)}, u32[]{:S(2)}) collective-permute-start(bf16[256,1664]{1,0:T(8,128)(2,1)} %fusion.47), channel_id=1, source_target_pairs={{0,32},{32,64},{64,96},{96,0},{1,33},{33,65},{65,97},{97,1},{2,34}... | collective-permute-start | bytes 2555912 | tf_op jit(solution)/shard_map/ppermute | solution.py:17
  36.2 20.0 %collective-permute-start.1 = (bf16[256,1664]{1,0:T(8,128)(2,1)S(1)}, bf16[256,1664]{1,0:T(8,128)(2,1)S(1)}, u32[]{:S(2)}, u32[]{:S(2)}) collective-permute-start(bf16[256,1664]{1,0:T(8,128)(2,1)S(1)} %collective-permute-done), channel_id=1, source_target_pairs={{0,32},{32,64},{64,96},{96,0},{1,33},{33,65},{65,97},{97,1},{2,34}... | collective-permute-start | bytes 2555912 | tf_op jit(solution)/shard_map/ppermute | solution.py:17
  36.6 23.0 %collective-permute-start.2 = (bf16[256,1664]{1,0:T(8,128)(2,1)}, bf16[256,1664]{1,0:T(8,128)(2,1)S(1)}, u32[]{:S(2)}, u32[]{:S(2)}) collective-permute-start(bf16[256,1664]{1,0:T(8,128)(2,1)} %fusion.47), channel_id=1, source_target_pairs={{0,96},{32,0},{64,32},{96,64},{1,97},{33,1},{65,33},{97,65},{2,98}... | collective-permute-start | bytes 2555912 | tf_op jit(solution)/shard_map/ppermute | solution.py:19
  58.2 50.4 %copy-start.15 = (f32[3,416]{1,0:T(4,128)S(1)}, f32[3,416]{1,0:T(4,128)}, u32[]{:S(2)}) copy-start(f32[3,416]{1,0:T(4,128)} %param.29) | copy-start | bytes 14980
  120.5 17.4 %copy-start.4 = (bf16[1664,416]{1,0:T(8,128)(2,1)S(1)}, bf16[1664,416]{1,0:T(8,128)(2,1)}, u32[]{:S(2)}) copy-start(bf16[1664,416]{1,0:T(8,128)(2,1)} %reshape.179) | copy-start | bytes 4153348
  138.0 42.9 %copy-start.5 = (f32[1664]{0:T(1024)S(1)}, f32[1664]{0:T(1024)}, u32[]{:S(2)}) copy-start(f32[1664]{0:T(1024)} %param.31) | copy-start | bytes 19972
  141.9 42.2 %copy-start.10 = (f32[1664]{0:T(1024)S(1)}, f32[1664]{0:T(1024)}, u32[]{:S(2)}) copy-start(f32[1664]{0:T(1024)} %param.33) | copy-start | bytes 19972
  141.9 42.2 %copy-start.11 = (f32[1664]{0:T(1024)S(1)}, f32[1664]{0:T(1024)}, u32[]{:S(2)}) copy-start(f32[1664]{0:T(1024)} %param.32) | copy-start | bytes 19972
  141.9 86.3 %all-gather.8.cloned.1.call-start = ((), (), s32[]{:S(2)}) async-start(), calls=%async_computation.4 | async-start | bytes 4259840 | tf_op jit(solution)/shard_map/all_gather | solution.py:103
  186.7 164.6 %all-reduce.2.cloned.1.call-start = ((), (), s32[]{:S(2)}) async-start(), calls=%async_computation.5 | async-start | bytes 6815744 | tf_op jit(solution)/shard_map/psum | solution.py:114
  186.8 52.8 %copy-start.16 = (f32[2048]{0:T(1024)S(1)}, f32[2048]{0:T(1024)}, u32[]{:S(2)}) copy-start(f32[2048]{0:T(1024)} %param.35) | copy-start | bytes 24580
  239.6 28.7 %copy-start.3 = (bf16[256,1664]{1,0:T(8,128)(2,1)S(1)}, bf16[256,1664]{1,0:T(8,128)(2,1)}, u32[]{:S(2)}) copy-start(bf16[256,1664]{1,0:T(8,128)(2,1)} %reduce-scatter.2.cloned.1.call-done) | copy-start | bytes 2555908
  270.9 80.4 %copy-start.8 = (f32[1664]{0:T(1024)S(1)}, f32[1664]{0:T(1024)}, u32[]{:S(2)}) copy-start(f32[1664]{0:T(1024)} %param.37) | copy-start | bytes 19972
  271.0 133.0 %all-gather.10.cloned.1.call-start = ((), (), s32[]{:S(2)}) async-start(), calls=%async_computation.6 | async-start | bytes 7028736 | tf_op jit(solution)/shard_map/all_gather | solution.py:125
  271.6 85.8 %copy-start.12 = (f32[1664]{0:T(1024)S(1)}, f32[1664]{0:T(1024)}, u32[]{:S(2)}) copy-start(f32[1664]{0:T(1024)} %param.39) | copy-start | bytes 19972
  271.6 85.8 %copy-start.13 = (f32[1664]{0:T(1024)S(1)}, f32[1664]{0:T(1024)}, u32[]{:S(2)}) copy-start(f32[1664]{0:T(1024)} %param.38) | copy-start | bytes 19972
  351.3 6.1 %copy-start.2 = (bf16[1024,1664]{1,0:T(8,128)(2,1)S(1)}, bf16[1024,1664]{1,0:T(8,128)(2,1)}, u32[]{:S(2)}) copy-start(bf16[1024,1664]{1,0:T(8,128)(2,1)} %all-reduce.2.cloned.1.call-done) | copy-start | bytes 10223620
  365.1 38.8 %copy-start.17 = (f32[416]{0:T(512)S(1)}, f32[416]{0:T(512)}, u32[]{:S(2)}) copy-start(f32[416]{0:T(512)} %param.41) | copy-start | bytes 4996
  (3 other events, 10.1 us)
Sparse Core Ops, SparseCore 0:
  9.6 47.2 all-gather.11
  59.1 49.3 all-gather.5
  142.1 38.7 reduce-scatter.1
  186.8 41.3 all-gather.7
  271.1 80.1 all-reduce.1
  353.4 50.4 all-gather.9
